TPU v7x, 128 devices: a whole 4x4x4 slice. The times are simulated.
128 devices in a mesh: dp: 64 (over z, y, x), tensor: 2 (over core).
Axes of the slice: x: 4, y: 4, z: 4, core: 2. Of those that a mesh axis runs over, the one named last changes fastest.
Arguments:
- square_grad: float32 [32, 2359296], P(None, ('dp', 'tensor')), may hold values from -80 to 80
- square_state: float32 [32, 2359296], P(None, ('dp', 'tensor')), may hold values from -6 to 6
- swiglu_grad: float32 [24, 6291456], P(None, ('dp', 'tensor')), may hold values from -80 to 80
- swiglu_state: float32 [24, 6291456], P(None, ('dp', 'tensor')), may hold values from -6 to 6
- square_order: int32 [32], replicated, may hold values from 0 to 31, each once
- swiglu_order: int32 [24], replicated, may hold values from 0 to 23, each once
- owners: int32 [56], replicated, may hold values from 0 to 63, as said below
- vector_values: float32 [172032], P(('dp', 'tensor')), may hold values from -6 to 6
- vector_grad: float32 [172032], P(('dp', 'tensor')), may hold values from -6 to 6
- vector_first: float32 [172032], P(('dp', 'tensor')), may hold values from -4 to 4
- vector_second: float32 [172032], P(('dp', 'tensor')), may hold values from 0.01 to 1
- embed_values: float32 [8192, 1536], P('dp', 'tensor'), may hold values from -6 to 6
- embed_grad: float32 [8192, 1536], P('dp', 'tensor'), may hold values from -6 to 6
- embed_first: float32 [8192, 1536], P('dp', 'tensor'), may hold values from -4 to 4
- embed_second: float32 [8192, 1536], P('dp', 'tensor'), may hold values from 0.01 to 1
- embed_ranges: int32 [16, 2], replicated, may hold values from 0 to 8192, as said below
Outputs:
- square_next: float32 [32, 2359296], P(None, ('dp', 'tensor'))
- swiglu_next: float32 [24, 6291456], P(None, ('dp', 'tensor'))
- square_update: bfloat16 [32, 1536, 1536], P(None, 'dp', 'tensor')
- swiglu_update: bfloat16 [24, 1536, 4096], P(None, 'dp', 'tensor')
- owner_norms: float32 [64], P('dp')
- vector_step: float32 [172032], P(('dp', 'tensor'))
- first_vector: float32 [172032], P(('dp', 'tensor'))
- second_vector: float32 [172032], P(('dp', 'tensor'))
- embed_step: float32 [8192, 1536], P('dp', 'tensor')
- first_embed: float32 [8192, 1536], P('dp', 'tensor')
- second_embed: float32 [8192, 1536], P('dp', 'tensor')
Inputs may be any that keep to these rules, and one draw needn't show every extreme that they name: Different matrices have different owners. `square_order`: each matrix once. `swiglu_order`: each matrix once. `embed_ranges`: start < end in every row.
All inputs are finite; a program needn't handle non-finite values.
Results may differ from a plain program's by a relative error of at most 0.0065.
Values may be sent and summed in bfloat16 or wider, within the bound.
A program may use at most 128 MiB of HBM per device.

v0:
```python
import math
import jax
import jax.numpy as jnp
from jax import lax
from jax.sharding import PartitionSpec as P

D = 1536
FF = 4096
NS_STEPS = 2
QUINTIC_LINEAR = 3.4445
QUINTIC_CUBIC = -4.775
QUINTIC_FIFTH = 2.0315
MOMENTUM = 0.95
BIAS_FIRST = 1.0 - 0.9**10
BIAS_SECOND = 1.0 - 0.95**10


def momentum_terms(gradient, state):
    state_next = MOMENTUM * state + gradient
    return (state_next, (gradient + MOMENTUM * state_next).astype(jnp.bfloat16))


def adamw_terms(values, gradient, first, second):
    first_next = 0.9 * first + 0.1 * gradient
    second_next = 0.95 * second + 0.05 * gradient * gradient
    direction = (
        first_next / BIAS_FIRST / (jnp.sqrt(second_next / BIAS_SECOND) + 1e-08) + 0.1 * values
    )
    return (direction, first_next, second_next)


def table_lookup(table, positions):
    matches = positions[:, None] == jnp.arange(table.shape[0], dtype=jnp.int32)[None, :]
    return jnp.sum(jnp.where(matches, table[None, :], 0), axis=1)


def select_pieces(pieces, piece_owner, targets):
    matched = piece_owner[None, :] == targets[:, None]
    chosen = jnp.sum(
        jnp.where(matched, jnp.arange(piece_owner.shape[0], dtype=jnp.int32)[None, :], 0), axis=1
    )
    present = jnp.any(matched, axis=1)
    picked = jnp.where(present[:, None, None, None], pieces[chosen], jnp.zeros((), jnp.bfloat16))
    return (picked, chosen, present)


def local(
    square_grad,
    square_state,
    swiglu_grad,
    swiglu_state,
    square_order,
    swiglu_order,
    owners,
    vector_values,
    vector_grad,
    vector_first,
    vector_second,
    embed_values,
    embed_grad,
    embed_first,
    embed_second,
    embed_ranges,
):
    wide_count = lax.axis_size("dp")
    split_count = lax.axis_size("tensor")
    wide_index = lax.axis_index("dp")
    square_count = square_grad.shape[0]
    swiglu_count = swiglu_grad.shape[0]
    flat_rows = D // (wide_count * split_count)
    slot_width = FF // split_count
    square_width = D // split_count
    square_next, square_send = momentum_terms(square_grad, square_state)
    swiglu_next, swiglu_send = momentum_terms(swiglu_grad, swiglu_state)
    square_pieces = square_send.reshape(
        square_count, flat_rows, split_count, square_width
    ).transpose(0, 2, 1, 3)
    swiglu_pieces = swiglu_send.reshape(swiglu_count, flat_rows, split_count, slot_width).transpose(
        0, 2, 1, 3
    )
    square_owner = table_lookup(owners[:square_count], square_order)
    swiglu_owner = table_lookup(owners[square_count:], swiglu_order)
    targets = jnp.arange(wide_count, dtype=jnp.int32)
    square_mine = jnp.any(square_owner == wide_index)
    owned = square_mine | jnp.any(swiglu_owner == wide_index)
    factor = jnp.where(square_mine, jnp.float32(math.sqrt(D)), jnp.float32(math.sqrt(FF)))
    widened = jnp.pad(square_pieces, ((0, 0), (0, 0), (0, 0), (0, slot_width - square_width)))
    all_pieces = jnp.concatenate([widened, swiglu_pieces], axis=0)
    slot_owner = jnp.concatenate([square_owner, swiglu_owner])
    outgoing, chosen, present = select_pieces(all_pieces, slot_owner, targets)
    arrived = lax.all_to_all(
        outgoing.reshape(D, slot_width), ("dp", "tensor"), split_axis=0, concat_axis=0, tiled=True
    )
    iterate = arrived
    first_scale = jnp.float32(1.0)
    for round_index in range(NS_STEPS):
        current = iterate
        gram_part = lax.psum_scatter(
            jnp.einsum("rc,sc->rs", current, current, preferred_element_type=jnp.float32),
            "tensor",
            scatter_dimension=0,
            tiled=True,
        )
        if round_index == 0:
            squares_total = lax.psum(jnp.sum(gram_part * gram_part), "tensor")
            gram_scale = jnp.sqrt(squares_total) + 1e-06
            first_scale = gram_scale
        else:
            gram_scale = jnp.float32(1.0)
        normed_part = (gram_part / gram_scale).astype(jnp.bfloat16)
        squared = jnp.dot(
            normed_part,
            lax.all_gather(normed_part, "tensor", axis=0, tiled=True),
            preferred_element_type=jnp.float32,
        )
        polynomial = (
            QUINTIC_CUBIC * normed_part.astype(jnp.float32) + QUINTIC_FIFTH * squared
        ).astype(jnp.bfloat16)
        product = jnp.dot(
            lax.all_gather(polynomial, "tensor", axis=0, tiled=True),
            current,
            preferred_element_type=jnp.float32,
        )
        mixed = (QUINTIC_LINEAR * current.astype(jnp.float32) + product) / jnp.sqrt(gram_scale)
        if round_index == NS_STEPS - 1:
            iterate = (factor * mixed).astype(jnp.bfloat16)
        else:
            iterate = mixed.astype(jnp.bfloat16)
    returned = lax.all_to_all(
        iterate.reshape(wide_count, D // wide_count, slot_width),
        "dp",
        split_axis=0,
        concat_axis=0,
        tiled=True,
    )
    square_update = returned[owners[:square_count]][:, :, :square_width]
    swiglu_update = returned[owners[square_count:]]
    owner_norms = jnp.where(owned, 0.5 * jnp.log(first_scale), 0.0).reshape(1)
    vector_step, first_vector, second_vector = adamw_terms(
        vector_values, vector_grad, vector_first, vector_second
    )
    embed_rows = embed_values.shape[0]
    row_numbers = wide_index * embed_rows + jnp.arange(embed_rows, dtype=jnp.int32)
    inside = (row_numbers[:, None] >= embed_ranges[None, :, 0]) & (
        row_numbers[:, None] < embed_ranges[None, :, 1]
    )
    row_live = jnp.sum(inside.astype(jnp.int32), axis=1) > 0
    direction, first_next, second_next = adamw_terms(
        embed_values, embed_grad, embed_first, embed_second
    )
    embed_step = jnp.where(row_live[:, None], direction, 0.0)
    first_embed = jnp.where(row_live[:, None], first_next, embed_first)
    second_embed = jnp.where(row_live[:, None], second_next, embed_second)
    return (
        square_next,
        swiglu_next,
        square_update,
        swiglu_update,
        owner_norms,
        vector_step,
        first_vector,
        second_vector,
        embed_step,
        first_embed,
        second_embed,
    )


def solution(mesh):
    placed = (
        P(None, ("dp", "tensor")),
        P(None, ("dp", "tensor")),
        P(None, ("dp", "tensor")),
        P(None, ("dp", "tensor")),
        P(),
        P(),
        P(),
        P(("dp", "tensor")),
        P(("dp", "tensor")),
        P(("dp", "tensor")),
        P(("dp", "tensor")),
        P("dp", "tensor"),
        P("dp", "tensor"),
        P("dp", "tensor"),
        P("dp", "tensor"),
        P(),
    )
    return jax.shard_map(
        local,
        mesh=mesh,
        in_specs=placed,
        out_specs=(
            P(None, ("dp", "tensor")),
            P(None, ("dp", "tensor")),
            P(None, "dp", "tensor"),
            P(None, "dp", "tensor"),
            P("dp"),
            P(("dp", "tensor")),
            P(("dp", "tensor")),
            P(("dp", "tensor")),
            P("dp", "tensor"),
            P("dp", "tensor"),
            P("dp", "tensor"),
        ),
        check_vma=False,
    )
```

profile of v0, /device:TPU:4, one launch (start us, length us, event | category | flops | bytes accessed | tf_op | source)
XLA Modules:
  0.0 515.0 jit_solution(1465619128677415151)
XLA Ops:
  7.2 0.0 reduce-scatter.3.cloned.1.call-start
  7.2 0.7 compare_select_fusion.1
  8.0 0.7 compare_select_fusion.2
  8.6 0.8 select_reduce_fusion.2
  9.5 0.8 select_reduce_fusion.1
  10.3 0.1 pad_add_fusion
  10.4 0.1 select_reduce_fusion
  10.5 0.3 copy-done.11
  10.8 0.1 fusion.4
  10.9 4.2 add_convert_fusion.3
  15.1 0.9 reshape.74
  16.0 7.5 %add_convert_fusion.2 = (bf16[24,49152]{1,0:T(8,128)(2,1)}, f32[24,49152]{1,0:T(8,128)}) fusion(f32[24,49152]{1,0:T(8,128)} %param.18, f32[24,49152]{1,0:T(8,128)} %param.19), kind=kLoop, calls=%fused_computation.12 | loop fusion | flops 5898240 | bytes 16515072 | tf_op jit(solution)/shard_map/convert_element_type | solution.py:20
  23.5 3.5 reshape.75
  27.0 5.3 %fusion = bf16[56,2,12,2048]{3,1,2,0:T(2,128)(2,1)} fusion(bf16[32,2,12,768]{3,1,2,0:T(2,128)(2,1)S(1)} %bitcast.28, bf16[24,2,12,2048]{3,1,2,0:T(2,128)(2,1)S(1)} %bitcast.26), kind=kLoop, calls=%fused_computation.7 | loop fusion | flops 16515072 | bytes 9043968 | tf_op jit(solution)/shard_map/concatenate | solution.py:88
  32.3 17.6 %gather_fusion = bf16[64,2,12,2048]{3,1,2,0:T(2,128)(2,1)} fusion(bf16[56,2,12,2048]{3,1,2,0:T(2,128)(2,1)} %fusion, s32[1024]{0:T(1024)S(1)} %pad_clamp_fusion.2), kind=kCustom, calls=%fused_computation | custom fusion | bytes 12583168 | tf_op jit(solution)/shard_map/gather | solution.py:43
  49.9 9.4 %copy.29 = bf16[64,2,12,2048]{3,2,1,0:T(8,128)(2,1)} copy(bf16[64,2,12,2048]{3,1,2,0:T(2,128)(2,1)} %gather_fusion) | data formatting | bytes 12582912 | tf_op jit(solution)/shard_map/gather | solution.py:43
  59.3 0.1 broadcast_in_dim.99
  59.4 0.2 broadcast_in_dim.100
  59.5 7.2 %bitcast_select_fusion = bf16[128,12,2048]{2,1,0:T(8,128)(2,1)} fusion(bf16[64,2,12,2048]{3,2,1,0:T(8,128)(2,1)} %copy.29, pred[128]{0:T(512)(128)(4,1)S(1)} %broadcast_in_dim.100), kind=kLoop, calls=%fused_computation.6 | loop fusion | flops 3145728 | bytes 12583040 | tf_op jit(solution)/shard_map/jit(_where)/select_n | solution.py:43
  66.8 107.0 %all_to_all.14 = bf16[128,12,2048]{2,1,0:T(8,128)(2,1)} all-to-all(bf16[128,12,2048]{2,1,0:T(8,128)(2,1)} %bitcast_select_fusion), channel_id=1, replica_groups=mesh['dp'=64,'tensor'=2] {'dp','tensor'}, dimensions={0} | all-to-all | bytes 12582912 | tf_op jit(solution)/shard_map/all_to_all | solution.py:91
  173.8 10.7 %all_to_all.10 = bf16[1536,2048]{1,0:T(8,128)(2,1)} reshape(bf16[128,12,2048]{2,1,0:T(8,128)(2,1)} %all_to_all.14) | data formatting | bytes 12582912 | tf_op jit(solution)/shard_map/all_to_all | solution.py:91
  184.5 16.2 %fusion.8 = f32[1536,1536]{1,0:T(8,128)} fusion(bf16[1536,2048]{1,0:T(8,128)(2,1)} %all_to_all.10), kind=kOutput, calls=%fused_computation.48 | convolution fusion | flops 9663676416 | bytes 15728640 | tf_op jit(solution)/shard_map/rc,sc->rs/dot_general | solution.py:99
  200.7 0.0 reduce-scatter.3.cloned.1.call-update
  200.7 0.0 all-gather.5.cloned.1.call-start
  200.8 18.6 %reduce-scatter.3.cloned.1.call-done = f32[768,1536]{1,0:T(8,128)} async-done(((f32[1536,1536]{1,0:T(8,128)}), f32[768,1536]{1,0:T(8,128)}) %reduce-scatter.3.cloned.1.call-update) | async-done | bytes 4718608 | tf_op jit(solution)/shard_map/reduce_scatter | solution.py:98
  219.4 4.2 multiply_reduce_fusion
  223.5 3.1 psum.7
  227.3 4.3 divide_convert_fusion.1
  231.6 0.0 all-gather.5.cloned.1.call-update
  231.6 0.0 all-gather.7.cloned.1.call-start
  231.7 18.6 %all-gather.5.cloned.1.call-done = bf16[1536,1536]{1,0:T(8,128)(2,1)} async-done(((bf16[768,1536]{1,0:T(8,128)(2,1)}), bf16[1536,1536]{1,0:T(8,128)(2,1)}) %all-gather.5.cloned.1.call-update) | async-done | bytes 4718608 | tf_op jit(solution)/shard_map/all_gather | solution.py:113
  250.3 9.1 %add_convert_fusion.1 = bf16[768,1536]{1,0:T(8,128)(2,1)} fusion(bf16[768,1536]{1,0:T(8,128)(2,1)} %divide_convert_fusion.1, bf16[1536,1536]{1,0:T(8,128)(2,1)} %all-gather.5.cloned.1.call-done), kind=kOutput, calls=%fused_computation.9 | convolution fusion | flops 3629776896 | bytes 9437184 | tf_op jit(solution)/shard_map/dot_general | solution.py:111
  259.4 0.0 all-gather.7.cloned.1.call-update
  259.4 0.2 reduce-scatter.5.cloned.1.call-start
  259.7 18.4 %all-gather.7.cloned.1.call-done = bf16[1536,1536]{1,0:T(8,128)(2,1)} async-done(((bf16[768,1536]{1,0:T(8,128)(2,1)}), bf16[1536,1536]{1,0:T(8,128)(2,1)}) %all-gather.7.cloned.1.call-update) | async-done | bytes 4718608 | tf_op jit(solution)/shard_map/all_gather | solution.py:120
  278.1 14.9 %divide_convert_fusion = bf16[1536,2048]{1,0:T(8,128)(2,1)S(1)} fusion(bf16[1536,2048]{1,0:T(8,128)(2,1)} %all_to_all.10, bf16[1536,1536]{1,0:T(8,128)(2,1)} %all-gather.7.cloned.1.call-done, f32[]{:T(128)S(6)} %sqrt.13), kind=kOutput, calls=%fused_computation.5 | convolution fusion | flops 9679405056 | bytes 17301508 | tf_op jit(solution)/shard_map/dot_general | solution.py:119
  293.0 2.7 copy-done.13
  295.6 12.7 %fusion.9 = f32[1536,1536]{1,0:T(8,128)} fusion(bf16[1536,2048]{1,0:T(8,128)(2,1)S(1)} %divide_convert_fusion), kind=kOutput, calls=%fused_computation.49 | convolution fusion | flops 9663676416 | bytes 15728640 | tf_op jit(solution)/shard_map/rc,sc->rs/dot_general | solution.py:99
  308.4 0.0 reduce-scatter.5.cloned.1.call-update
  308.4 0.0 all-gather.9.cloned.1.call-start
  308.4 22.0 %reduce-scatter.5.cloned.1.call-done = f32[768,1536]{1,0:T(8,128)} async-done(((f32[1536,1536]{1,0:T(8,128)}), f32[768,1536]{1,0:T(8,128)}) %reduce-scatter.5.cloned.1.call-update) | async-done | bytes 4718608 | tf_op jit(solution)/shard_map/reduce_scatter | solution.py:98
  330.4 4.0 convert_element_type.49
  334.4 0.0 all-gather.9.cloned.1.call-update
  334.5 0.0 copy-start.12
  334.5 0.3 all-gather.11.cloned.1.call-start
  334.7 18.5 %all-gather.9.cloned.1.call-done = bf16[1536,1536]{1,0:T(8,128)(2,1)} async-done(((bf16[768,1536]{1,0:T(8,128)(2,1)}), bf16[1536,1536]{1,0:T(8,128)(2,1)}) %all-gather.9.cloned.1.call-update) | async-done | bytes 4718608 | tf_op jit(solution)/shard_map/all_gather | solution.py:113
  353.2 9.1 %add_convert_fusion = bf16[768,1536]{1,0:T(8,128)(2,1)} fusion(bf16[768,1536]{1,0:T(8,128)(2,1)} %convert_element_type.49, bf16[1536,1536]{1,0:T(8,128)(2,1)} %all-gather.9.cloned.1.call-done), kind=kOutput, calls=%fused_computation.8 | convolution fusion | flops 3629776896 | bytes 9437184 | tf_op jit(solution)/shard_map/dot_general | solution.py:111
  362.3 0.0 all-gather.11.cloned.1.call-update
  362.3 0.6 compare_reduce_fusion.1
  363.6 17.4 %all-gather.11.cloned.1.call-done = bf16[1536,1536]{1,0:T(8,128)(2,1)} async-done(((bf16[768,1536]{1,0:T(8,128)(2,1)}), bf16[1536,1536]{1,0:T(8,128)(2,1)}) %all-gather.11.cloned.1.call-update) | async-done | bytes 4718608 | tf_op jit(solution)/shard_map/all_gather | solution.py:120
  380.9 16.6 %multiply_convert_fusion = bf16[1536,2048]{1,0:T(8,128)(2,1)} fusion(bf16[1536,2048]{1,0:T(8,128)(2,1)} %copy-done.13, bf16[1536,1536]{1,0:T(8,128)(2,1)} %all-gather.11.cloned.1.call-done, f32[]{:T(128)S(6)} %select_n.54), kind=kOutput, calls=%fused_computation.4 | convolution fusion | flops 9679405056 | bytes 17301508 | tf_op jit(solution)/shard_map/dot_general | solution.py:119
  397.6 0.0 copy-start.5
  397.6 0.0 copy-start.6
  397.6 0.0 copy-start.1
  397.6 0.0 copy-start.2
  397.6 10.7 %all-to-all-start.1 = ((bf16[64,24,2048]{2,1,0:T(8,128)(2,1)}), bf16[64,24,2048]{2,1,0:T(8,128)(2,1)}, u32[]{:S(2)}, u32[]{:S(2)}) async-start(bf16[64,24,2048]{2,1,0:T(8,128)(2,1)} %bitcast.27), calls=%async_computation.3 | async-start | bytes 12582912 | tf_op jit(solution)/shard_map/all_to_all | solution.py:129
  408.4 0.6 compare_reduce_fusion
  410.4 0.1 convert_reduce_fusion
  410.5 0.6 multiply_add_fusion.3
  411.1 1.4 fusion.3
  412.6 84.5 %all-to-all-done.1 = bf16[64,24,2048]{2,1,0:T(8,128)(2,1)} async-done(((bf16[64,24,2048]{2,1,0:T(8,128)(2,1)}), bf16[64,24,2048]{2,1,0:T(8,128)(2,1)}, u32[]{:S(2)}, u32[]{:S(2)}) %all-to-all-start.1) | async-done | bytes 6291488 | tf_op jit(solution)/shard_map/all_to_all | solution.py:129
  497.1 3.5 gather_fusion.1
  500.7 1.1 slice.28
  501.8 5.0 gather_fusion.2
  (28 shorter events, 0.1 us)
Async XLA Ops:
  7.2 212.2 %reduce-scatter.3.cloned.1.call-start = ((), (), s32[]{:S(2)}) async-start(), calls=%async_computation.4 | async-start | bytes 14155776 | tf_op jit(solution)/shard_map/reduce_scatter | solution.py:98
  9.4 1.0 copy-start.9
  10.3 0.5 copy-start.11
  200.7 49.6 %all-gather.5.cloned.1.call-start = ((), (), s32[]{:S(2)}) async-start(), calls=%async_computation.5 | async-start | bytes 7077888 | tf_op jit(solution)/shard_map/all_gather | solution.py:113
  231.6 46.4 %all-gather.7.cloned.1.call-start = ((), (), s32[]{:S(2)}) async-start(), calls=%async_computation.6 | async-start | bytes 7077888 | tf_op jit(solution)/shard_map/all_gather | solution.py:120
  259.4 71.0 %reduce-scatter.5.cloned.1.call-start = ((), (), s32[]{:S(2)}) async-start(), calls=%async_computation.7 | async-start | bytes 14155776 | tf_op jit(solution)/shard_map/reduce_scatter | solution.py:98
  293.0 2.7 copy-start.13
  308.4 44.8 %all-gather.9.cloned.1.call-start = ((), (), s32[]{:S(2)}) async-start(), calls=%async_computation.8 | async-start | bytes 7077888 | tf_op jit(solution)/shard_map/all_gather | solution.py:113
  334.5 27.8 %copy-start.12 = (s32[32]{0:T(128)S(1)}, s32[32]{0:T(128)}, u32[]{:S(2)}) copy-start(s32[32]{0:T(128)} %copy-done.11) | copy-start | bytes 388
  334.5 46.5 %all-gather.11.cloned.1.call-start = ((), (), s32[]{:S(2)}) async-start(), calls=%async_computation.9 | async-start | bytes 7077888 | tf_op jit(solution)/shard_map/all_gather | solution.py:120
  397.5 10.8 %copy-start.10 = (s32[24]{0:T(128)S(1)}, s32[24]{0:T(128)}, u32[]{:S(2)}) copy-start(s32[24]{0:T(128)} %copy-done.9) | copy-start | bytes 292
  397.6 12.8 %copy-start.8 = (s32[16,2]{0,1:T(2,128)S(1)}, s32[16,2]{0,1:T(2,128)}, u32[]{:S(2)}) copy-start(s32[16,2]{0,1:T(2,128)} %param.31) | copy-start | bytes 388
  397.6 12.9 %copy-start.4 = (f32[1344]{0:T(1024)S(1)}, f32[1344]{0:T(1024)}, u32[]{:S(2)}) copy-start(f32[1344]{0:T(1024)} %param.23) | copy-start | bytes 16132
  397.6 12.9 %copy-start.5 = (f32[1344]{0:T(1024)S(1)}, f32[1344]{0:T(1024)}, u32[]{:S(2)}) copy-start(f32[1344]{0:T(1024)} %param.24) | copy-start | bytes 16132
  397.6 12.9 %copy-start.6 = (f32[1344]{0:T(1024)S(1)}, f32[1344]{0:T(1024)}, u32[]{:S(2)}) copy-start(f32[1344]{0:T(1024)} %param.25) | copy-start | bytes 16132
  397.6 12.9 %copy-start.7 = (f32[1344]{0:T(1024)S(1)}, f32[1344]{0:T(1024)}, u32[]{:S(2)}) copy-start(f32[1344]{0:T(1024)} %param.26) | copy-start | bytes 16132
  397.6 13.5 %copy-start = (f32[128,768]{1,0:T(8,128)S(1)}, f32[128,768]{1,0:T(8,128)}, u32[]{:S(2)}) copy-start(f32[128,768]{1,0:T(8,128)} %param.30) | copy-start | bytes 1179652
  397.6 13.5 %copy-start.1 = (f32[128,768]{1,0:T(8,128)S(1)}, f32[128,768]{1,0:T(8,128)}, u32[]{:S(2)}) copy-start(f32[128,768]{1,0:T(8,128)} %param.28) | copy-start | bytes 1179652
  397.6 13.5 %copy-start.2 = (f32[128,768]{1,0:T(8,128)S(1)}, f32[128,768]{1,0:T(8,128)}, u32[]{:S(2)}) copy-start(f32[128,768]{1,0:T(8,128)} %param.27) | copy-start | bytes 1179652
  397.6 13.5 %copy-start.3 = (f32[128,768]{1,0:T(8,128)S(1)}, f32[128,768]{1,0:T(8,128)}, u32[]{:S(2)}) copy-start(f32[128,768]{1,0:T(8,128)} %param.29) | copy-start | bytes 1179652
  397.6 99.5 %all-to-all-start.1 = ((bf16[64,24,2048]{2,1,0:T(8,128)(2,1)}), bf16[64,24,2048]{2,1,0:T(8,128)(2,1)}, u32[]{:S(2)}, u32[]{:S(2)}) async-start(bf16[64,24,2048]{2,1,0:T(8,128)(2,1)} %bitcast.27), calls=%async_computation.3 | async-start | bytes 12582912 | tf_op jit(solution)/shard_map/all_to_all | solution.py:129
Sparse Core Ops, SparseCore 0:
  200.8 18.4 reduce-scatter.2
  231.8 18.5 all-gather.4
  259.5 18.4 all-gather.6
  308.5 21.8 reduce-scatter.4
  334.6 18.5 all-gather.8
  362.4 18.4 all-gather.10
where the time goes:
time: 524 us; the launch traced here: 515 us
  waiting for transfers between devices  198 us (38%)
  blocking collectives  110 us (21%)
  matrix products  78.6 us (15%)
  local copies, waits for them, and re-layouts  55 us (10%)
  other arithmetic  43.4 us (8%)
  between operations  18.5 us (4%)
  starting transfers between devices  11.3 us (2%)
    all_to_all x1, blocking collectives, local(): lax.all_to_all(outgoing.reshape(D, slot_width), ('dp', 'tensor'), split_a...  107 us
    all_to_all x1, waiting for transfers between devices, local(): lax.all_to_all(iterate.reshape(wide_count, D // wide_count, slot_width),...  84.5 us
    reduce_scatter x2, waiting for transfers between devices, local(): lax.psum_scatter(jnp.einsum('rc,sc->rs', current, current, preferred_elem...  40.6 us
    all_gather x2, waiting for transfers between devices, local(): lax.all_gather(normed_part, 'tensor', axis=0, tiled=True)  37.1 us
    all_gather x2, waiting for transfers between devices, local(): lax.all_gather(polynomial, 'tensor', axis=0, tiled=True)  35.7 us
    dot_general x2, matrix products, local(): jnp.dot(lax.all_gather(polynomial, 'tensor', axis=0, tiled=True), current...  31.5 us
    dot_general x2, matrix products, local(): jnp.einsum('rc,sc->rs', current, current, preferred_element_type=jnp.floa...  29 us
    gather x2, local copies, waits for them, and re-layouts, select_pieces(): pieces[chosen]  27 us
  transfers between devices with their start and end apart: 7, of which 7 were waited for; matrix products, arithmetic and copies ran while one was open for 1% of the time, Pallas kernels for 0%

commit v1 on v0

--- a/solution.py
+++ b/solution.py
@@ -110,7 +110,10 @@
         normed_part = (gram_part / gram_scale).astype(jnp.bfloat16)
         squared = jnp.dot(
             normed_part,
-            lax.all_gather(normed_part, "tensor", axis=0, tiled=True),
+            jnp.concatenate(
+                lax.all_to_all(jnp.stack([normed_part] * lax.axis_size("tensor")), "tensor", 0, 0),
+                axis=0,
+            ),
             preferred_element_type=jnp.float32,
         )
         polynomial = (

time: 524 us -> 492 us (0.939)
  waiting for transfers between devices: 198 us -> 161 us
  blocking collectives: 110 us -> 126 us
  matrix products: 78.6 us -> 71.1 us
    all_gather x2 -> x0, waiting for transfers between devices: 37.1 us -> none  [local(): lax.all_gather(normed_part, 'tensor', axis=0, tiled=True)]
    all_to_all x0 -> x2, blocking collectives: none -> 15.7 us  [local(): lax.all_to_all(jnp.stack([normed_part] * lax.axis_size('tensor')), 'tenso...]
    convert_element_type x2 -> x0, other arithmetic: 8.31 us -> none  [local(): normed_part = (gram_part / gram_scale).astype(jnp.bfloat16)]
    dot_general x2, matrix products: 18.2 us -> 10.4 us  [local(): jnp.dot(normed_part, jnp.concatenate(lax.all_to_all(jnp.stack([normed_par...]
    another operation x0 -> x4, other arithmetic: none -> 6.32 us  [local(): jnp.stack([normed_part] * lax.axis_size('tensor'))]
  transfers between devices with their start and end apart: 7 -> 5, of which waited for: 7 -> 5; matrix products, arithmetic and copies ran while one was open for 1% -> 1% of each run, Pallas kernels for 0% -> 0%
where the time goes in v1:
time: 492 us; the launch traced here: 483 us
  waiting for transfers between devices  161 us (33%)
  blocking collectives  126 us (26%)
  matrix products  71.1 us (14%)
  local copies, waits for them, and re-layouts  55 us (11%)
  other arithmetic  41.4 us (8%)
  between operations  18.2 us (4%)
  starting transfers between devices  11.3 us (2%)
    all_to_all x1, blocking collectives, local(): lax.all_to_all(outgoing.reshape(D, slot_width), ('dp', 'tensor'), split_a...  107 us
    all_to_all x1, waiting for transfers between devices, local(): lax.all_to_all(iterate.reshape(wide_count, D // wide_count, slot_width),...  84.5 us
    reduce_scatter x2, waiting for transfers between devices, local(): lax.psum_scatter(jnp.einsum('rc,sc->rs', current, current, preferred_elem...  40.6 us
    all_gather x2, waiting for transfers between devices, local(): lax.all_gather(polynomial, 'tensor', axis=0, tiled=True)  35.5 us
    dot_general x2, matrix products, local(): jnp.dot(lax.all_gather(polynomial, 'tensor', axis=0, tiled=True), current...  31.5 us
    dot_general x2, matrix products, local(): jnp.einsum('rc,sc->rs', current, current, preferred_element_type=jnp.floa...  29.2 us
    gather x2, local copies, waits for them, and re-layouts, select_pieces(): pieces[chosen]  27 us
    all_to_all x2, blocking collectives, local(): lax.all_to_all(jnp.stack([normed_part] * lax.axis_size('tensor')), 'tenso...  15.7 us
  transfers between devices with their start and end apart: 5, of which 5 were waited for; matrix products, arithmetic and copies ran while one was open for 1% of the time, Pallas kernels for 0%

profile of v1, /device:TPU:4, one launch (start us, length us, event | category | flops | bytes accessed | tf_op | source)
XLA Modules:
  0.0 483.4 jit_solution(14961899683188364699)
XLA Ops:
  7.2 0.0 reduce-scatter.3.cloned.1.call-start
  7.2 0.7 compare_select_fusion.1
  8.0 0.7 compare_select_fusion.2
  8.6 0.8 select_reduce_fusion.2
  9.5 0.8 select_reduce_fusion.1
  10.3 0.1 pad_add_fusion
  10.4 0.1 select_reduce_fusion
  10.5 0.3 copy-done.11
  10.8 0.1 fusion.5
  10.9 4.2 add_convert_fusion.3
  15.1 0.9 reshape.80
  16.0 7.5 %add_convert_fusion.2 = (bf16[24,49152]{1,0:T(8,128)(2,1)}, f32[24,49152]{1,0:T(8,128)}) fusion(f32[24,49152]{1,0:T(8,128)} %param.18, f32[24,49152]{1,0:T(8,128)} %param.19), kind=kLoop, calls=%fused_computation.14 | loop fusion | flops 5898240 | bytes 16515072 | tf_op jit(solution)/shard_map/convert_element_type | solution.py:20
  23.5 3.5 reshape.81
  27.0 5.3 %fusion = bf16[56,2,12,2048]{3,1,2,0:T(2,128)(2,1)} fusion(bf16[32,2,12,768]{3,1,2,0:T(2,128)(2,1)S(1)} %bitcast.34, bf16[24,2,12,2048]{3,1,2,0:T(2,128)(2,1)S(1)} %bitcast.32), kind=kLoop, calls=%fused_computation.7 | loop fusion | flops 16515072 | bytes 9043968 | tf_op jit(solution)/shard_map/concatenate | solution.py:88
  32.3 17.6 %gather_fusion = bf16[64,2,12,2048]{3,1,2,0:T(2,128)(2,1)} fusion(bf16[56,2,12,2048]{3,1,2,0:T(2,128)(2,1)} %fusion, s32[1024]{0:T(1024)S(1)} %pad_clamp_fusion.2), kind=kCustom, calls=%fused_computation | custom fusion | bytes 12583168 | tf_op jit(solution)/shard_map/gather | solution.py:43
  49.9 9.4 %copy.29 = bf16[64,2,12,2048]{3,2,1,0:T(8,128)(2,1)} copy(bf16[64,2,12,2048]{3,1,2,0:T(2,128)(2,1)} %gather_fusion) | data formatting | bytes 12582912 | tf_op jit(solution)/shard_map/gather | solution.py:43
  59.3 0.1 broadcast_in_dim.99
  59.4 0.2 broadcast_in_dim.100
  59.5 7.3 %bitcast_select_fusion = bf16[128,12,2048]{2,1,0:T(8,128)(2,1)} fusion(bf16[64,2,12,2048]{3,2,1,0:T(8,128)(2,1)} %copy.29, pred[128]{0:T(512)(128)(4,1)S(1)} %broadcast_in_dim.100), kind=kLoop, calls=%fused_computation.6 | loop fusion | flops 3145728 | bytes 12583040 | tf_op jit(solution)/shard_map/jit(_where)/select_n | solution.py:43
  66.8 106.8 %all_to_all.24 = bf16[128,12,2048]{2,1,0:T(8,128)(2,1)} all-to-all(bf16[128,12,2048]{2,1,0:T(8,128)(2,1)} %bitcast_select_fusion), channel_id=1, replica_groups=mesh['dp'=64,'tensor'=2] {'dp','tensor'}, dimensions={0} | all-to-all | bytes 12582912 | tf_op jit(solution)/shard_map/all_to_all | solution.py:91
  173.6 10.7 %all_to_all.16 = bf16[1536,2048]{1,0:T(8,128)(2,1)} reshape(bf16[128,12,2048]{2,1,0:T(8,128)(2,1)} %all_to_all.24) | data formatting | bytes 12582912 | tf_op jit(solution)/shard_map/all_to_all | solution.py:91
  184.3 16.3 %fusion.10 = f32[1536,1536]{1,0:T(8,128)} fusion(bf16[1536,2048]{1,0:T(8,128)(2,1)} %all_to_all.16), kind=kOutput, calls=%fused_computation.53 | convolution fusion | flops 9663676416 | bytes 15728640 | tf_op jit(solution)/shard_map/rc,sc->rs/dot_general | solution.py:99
  200.6 0.0 reduce-scatter.3.cloned.1.call-update
  200.6 0.0 all-gather.3.cloned.1.call-start
  200.7 18.6 %reduce-scatter.3.cloned.1.call-done = f32[768,1536]{1,0:T(8,128)} async-done(((f32[1536,1536]{1,0:T(8,128)}), f32[768,1536]{1,0:T(8,128)}) %reduce-scatter.3.cloned.1.call-update) | async-done | bytes 4718608 | tf_op jit(solution)/shard_map/reduce_scatter | solution.py:98
  219.3 4.2 multiply_reduce_fusion
  223.4 3.1 psum.7
  227.2 2.9 fusion.8
  230.1 0.4 pad_maximum_fusion
  230.5 7.8 %all_to_all.25 = bf16[2,768,1536]{2,1,0:T(8,128)(2,1)S(1)} all-to-all(bf16[2,768,1536]{2,1,0:T(8,128)(2,1)S(1)} %pad_maximum_fusion), channel_id=1, replica_groups=mesh['dp'=64,'tensor'=2] {'tensor'}, dimensions={0} | all-to-all | bytes 9437184 | tf_op jit(solution)/shard_map/all_to_all | solution.py:114
  238.3 5.2 %add_convert_fusion.1 = bf16[768,1536]{1,0:T(8,128)(2,1)} fusion(bf16[1536,1536]{1,0:T(8,128)(2,1)S(1)} %bitcast.37, f32[768,1536]{1,0:T(8,128)S(1)} %bitcast.31, f32[]{:T(128)S(6)} %add.103), kind=kOutput, calls=%fused_computation.11 | convolution fusion | flops 3634495488 | bytes 11796484 | tf_op jit(solution)/shard_map/dot_general | solution.py:111
  243.5 0.0 all-gather.3.cloned.1.call-update
  243.5 0.5 reduce-scatter.5.cloned.1.call-start
  244.1 18.1 %all-gather.3.cloned.1.call-done = bf16[1536,1536]{1,0:T(8,128)(2,1)} async-done(((bf16[768,1536]{1,0:T(8,128)(2,1)}), bf16[1536,1536]{1,0:T(8,128)(2,1)}) %all-gather.3.cloned.1.call-update) | async-done | bytes 4718608 | tf_op jit(solution)/shard_map/all_gather | solution.py:123
  262.2 14.9 %divide_convert_fusion = bf16[1536,2048]{1,0:T(8,128)(2,1)S(1)} fusion(bf16[1536,2048]{1,0:T(8,128)(2,1)} %all_to_all.16, bf16[1536,1536]{1,0:T(8,128)(2,1)} %all-gather.3.cloned.1.call-done, f32[]{:T(128)S(6)} %sqrt.13), kind=kOutput, calls=%fused_computation.5 | convolution fusion | flops 9679405056 | bytes 17301508 | tf_op jit(solution)/shard_map/dot_general | solution.py:122
  277.1 2.7 copy-done.13
  279.8 12.9 %fusion.11 = f32[1536,1536]{1,0:T(8,128)} fusion(bf16[1536,2048]{1,0:T(8,128)(2,1)S(1)} %divide_convert_fusion), kind=kOutput, calls=%fused_computation.54 | convolution fusion | flops 9663676416 | bytes 15728640 | tf_op jit(solution)/shard_map/rc,sc->rs/dot_general | solution.py:99
  292.7 0.0 reduce-scatter.5.cloned.1.call-update
  292.7 0.0 all-gather.5.cloned.1.call-start
  292.7 22.0 %reduce-scatter.5.cloned.1.call-done = f32[768,1536]{1,0:T(8,128)} async-done(((f32[1536,1536]{1,0:T(8,128)}), f32[768,1536]{1,0:T(8,128)}) %reduce-scatter.5.cloned.1.call-update) | async-done | bytes 4718608 | tf_op jit(solution)/shard_map/reduce_scatter | solution.py:98
  314.7 2.6 convert_bitcast_fusion
  317.3 0.4 pad_maximum_fusion.1
  317.8 7.9 %all_to_all.26 = bf16[2,768,1536]{2,1,0:T(8,128)(2,1)S(1)} all-to-all(bf16[2,768,1536]{2,1,0:T(8,128)(2,1)S(1)} %pad_maximum_fusion.1), channel_id=1, replica_groups=mesh['dp'=64,'tensor'=2] {'tensor'}, dimensions={0} | all-to-all | bytes 9437184 | tf_op jit(solution)/shard_map/all_to_all | solution.py:114
  325.7 5.2 %add_convert_fusion = bf16[768,1536]{1,0:T(8,128)(2,1)} fusion(bf16[1536,1536]{1,0:T(8,128)(2,1)S(1)} %bitcast.38, f32[768,1536]{1,0:T(8,128)S(1)} %bitcast.36), kind=kOutput, calls=%fused_computation.10 | convolution fusion | flops 3632136192 | bytes 11796480 | tf_op jit(solution)/shard_map/dot_general | solution.py:111
  331.0 0.0 all-gather.5.cloned.1.call-update
  331.0 0.6 compare_reduce_fusion.1
  332.3 17.4 %all-gather.5.cloned.1.call-done = bf16[1536,1536]{1,0:T(8,128)(2,1)} async-done(((bf16[768,1536]{1,0:T(8,128)(2,1)}), bf16[1536,1536]{1,0:T(8,128)(2,1)}) %all-gather.5.cloned.1.call-update) | async-done | bytes 4718608 | tf_op jit(solution)/shard_map/all_gather | solution.py:123
  349.7 16.6 %multiply_convert_fusion = bf16[1536,2048]{1,0:T(8,128)(2,1)} fusion(bf16[1536,2048]{1,0:T(8,128)(2,1)} %copy-done.13, bf16[1536,1536]{1,0:T(8,128)(2,1)} %all-gather.5.cloned.1.call-done, f32[]{:T(128)S(6)} %select_n.54), kind=kOutput, calls=%fused_computation.4 | convolution fusion | flops 9679405056 | bytes 17301508 | tf_op jit(solution)/shard_map/dot_general | solution.py:122
  366.3 0.0 copy-start.5
  366.3 0.0 copy-start.6
  366.3 0.0 copy-start.7
  366.3 0.0 copy-start
  366.4 0.0 copy-start.1
  366.4 0.0 copy-start.2
  366.4 0.0 copy-start.3
  366.4 10.7 %all-to-all-start.3 = ((bf16[64,24,2048]{2,1,0:T(8,128)(2,1)}), bf16[64,24,2048]{2,1,0:T(8,128)(2,1)}, u32[]{:S(2)}, u32[]{:S(2)}) async-start(bf16[64,24,2048]{2,1,0:T(8,128)(2,1)} %bitcast.33), calls=%async_computation.5 | async-start | bytes 12582912 | tf_op jit(solution)/shard_map/all_to_all | solution.py:132
  377.1 0.6 compare_reduce_fusion
  379.1 0.1 convert_reduce_fusion
  379.3 0.6 multiply_add_fusion.3
  379.9 1.4 fusion.4
  381.4 84.5 %all-to-all-done.3 = bf16[64,24,2048]{2,1,0:T(8,128)(2,1)} async-done(((bf16[64,24,2048]{2,1,0:T(8,128)(2,1)}), bf16[64,24,2048]{2,1,0:T(8,128)(2,1)}, u32[]{:S(2)}, u32[]{:S(2)}) %all-to-all-start.3) | async-done | bytes 6291488 | tf_op jit(solution)/shard_map/all_to_all | solution.py:132
  465.9 3.5 gather_fusion.1
  469.4 1.1 slice.28
  470.6 5.0 %gather_fusion.2 = bf16[24,24,2048]{2,1,0:T(8,128)(2,1)} fusion(bf16[64,24,2048]{2,1,0:T(8,128)(2,1)} %all-to-all-done.3, s32[1024]{0:T(1024)S(1)} %pad_clamp_fusion), kind=kCustom, calls=%fused_computation.2 | custom fusion | bytes 4718688 | tf_op jit(solution)/shard_map/gather | solution.py:140
  (36 shorter events, 0.1 us)
Async XLA Ops:
  7.2 212.1 %reduce-scatter.3.cloned.1.call-start = ((), (), s32[]{:S(2)}) async-start(), calls=%async_computation.6 | async-start | bytes 14155776 | tf_op jit(solution)/shard_map/reduce_scatter | solution.py:98
  9.4 1.0 copy-start.9
  10.3 0.5 copy-start.11
  200.6 61.6 %all-gather.3.cloned.1.call-start = ((), (), s32[]{:S(2)}) async-start(), calls=%async_computation.7 | async-start | bytes 7077888 | tf_op jit(solution)/shard_map/all_gather | solution.py:123
  230.1 8.2 %slice-start = ((s8[4718592]{0:T(1024)(128)(4,1)}), s8[524288]{0:T(1024)(128)(4,1)S(1)}, s32[]{:S(2)}) async-start(s8[4718592]{0:T(1024)(128)(4,1)} %bitcast.30), calls=%async_computation.10 | async-start | bytes 1048576
  230.5 7.8 %slice-start.1 = ((s8[4718592]{0:T(1024)(128)(4,1)}), s8[4194304]{0:T(1024)(128)(4,1)S(1)}, s32[]{:S(2)}) async-start(s8[4718592]{0:T(1024)(128)(4,1)} %bitcast.30), calls=%async_computation.11 | async-start | bytes 8388608
  243.5 71.2 %reduce-scatter.5.cloned.1.call-start = ((), (), s32[]{:S(2)}) async-start(), calls=%async_computation.8 | async-start | bytes 14155776 | tf_op jit(solution)/shard_map/reduce_scatter | solution.py:98
  277.1 2.7 copy-start.13
  292.7 57.0 %all-gather.5.cloned.1.call-start = ((), (), s32[]{:S(2)}) async-start(), calls=%async_computation.9 | async-start | bytes 7077888 | tf_op jit(solution)/shard_map/all_gather | solution.py:123
  317.3 8.4 %slice-start.2 = ((s8[4718592]{0:T(1024)(128)(4,1)}), s8[524288]{0:T(1024)(128)(4,1)S(1)}, s32[]{:S(2)}) async-start(s8[4718592]{0:T(1024)(128)(4,1)} %bitcast.35), calls=%async_computation.12 | async-start | bytes 1048576
  317.7 8.0 %slice-start.3 = ((s8[4718592]{0:T(1024)(128)(4,1)}), s8[4194304]{0:T(1024)(128)(4,1)S(1)}, s32[]{:S(2)}) async-start(s8[4718592]{0:T(1024)(128)(4,1)} %bitcast.35), calls=%async_computation.13 | async-start | bytes 8388608
  325.7 5.3 %copy-start.12 = (s32[32]{0:T(128)S(1)}, s32[32]{0:T(128)}, u32[]{:S(2)}) copy-start(s32[32]{0:T(128)} %copy-done.11) | copy-start | bytes 388
  366.3 10.8 %copy-start.10 = (s32[24]{0:T(128)S(1)}, s32[24]{0:T(128)}, u32[]{:S(2)}) copy-start(s32[24]{0:T(128)} %copy-done.9) | copy-start | bytes 292
  366.3 12.8 %copy-start.8 = (s32[16,2]{0,1:T(2,128)S(1)}, s32[16,2]{0,1:T(2,128)}, u32[]{:S(2)}) copy-start(s32[16,2]{0,1:T(2,128)} %param.31) | copy-start | bytes 388
  366.3 12.9 %copy-start.4 = (f32[1344]{0:T(1024)S(1)}, f32[1344]{0:T(1024)}, u32[]{:S(2)}) copy-start(f32[1344]{0:T(1024)} %param.23) | copy-start | bytes 16132
  366.3 12.9 %copy-start.5 = (f32[1344]{0:T(1024)S(1)}, f32[1344]{0:T(1024)}, u32[]{:S(2)}) copy-start(f32[1344]{0:T(1024)} %param.24) | copy-start | bytes 16132
  366.3 12.9 %copy-start.6 = (f32[1344]{0:T(1024)S(1)}, f32[1344]{0:T(1024)}, u32[]{:S(2)}) copy-start(f32[1344]{0:T(1024)} %param.25) | copy-start | bytes 16132
  366.3 12.9 %copy-start.7 = (f32[1344]{0:T(1024)S(1)}, f32[1344]{0:T(1024)}, u32[]{:S(2)}) copy-start(f32[1344]{0:T(1024)} %param.26) | copy-start | bytes 16132
  366.3 13.5 %copy-start = (f32[128,768]{1,0:T(8,128)S(1)}, f32[128,768]{1,0:T(8,128)}, u32[]{:S(2)}) copy-start(f32[128,768]{1,0:T(8,128)} %param.30) | copy-start | bytes 1179652
  366.4 13.5 %copy-start.1 = (f32[128,768]{1,0:T(8,128)S(1)}, f32[128,768]{1,0:T(8,128)}, u32[]{:S(2)}) copy-start(f32[128,768]{1,0:T(8,128)} %param.28) | copy-start | bytes 1179652
  366.4 13.5 %copy-start.2 = (f32[128,768]{1,0:T(8,128)S(1)}, f32[128,768]{1,0:T(8,128)}, u32[]{:S(2)}) copy-start(f32[128,768]{1,0:T(8,128)} %param.27) | copy-start | bytes 1179652
  366.4 13.5 %copy-start.3 = (f32[128,768]{1,0:T(8,128)S(1)}, f32[128,768]{1,0:T(8,128)}, u32[]{:S(2)}) copy-start(f32[128,768]{1,0:T(8,128)} %param.29) | copy-start | bytes 1179652
  366.4 99.5 %all-to-all-start.3 = ((bf16[64,24,2048]{2,1,0:T(8,128)(2,1)}), bf16[64,24,2048]{2,1,0:T(8,128)(2,1)}, u32[]{:S(2)}, u32[]{:S(2)}) async-start(bf16[64,24,2048]{2,1,0:T(8,128)(2,1)} %bitcast.33), calls=%async_computation.5 | async-start | bytes 12582912 | tf_op jit(solution)/shard_map/all_to_all | solution.py:132
Sparse Core Ops, SparseCore 0:
  200.7 18.4 reduce-scatter.2
  243.7 18.5 all-gather.2
  292.8 21.8 reduce-scatter.4
  331.1 18.5 all-gather.4
